TPU v7x, 128 devices: a whole 4x4x4 slice. The times are simulated.
128 devices in a mesh: cluster: 8 (over x, core), row: 16 (over z, y).
Axes of the slice: x: 4, y: 4, z: 4, core: 2. Of those that a mesh axis runs over, the one named last changes fastest.
Arguments:
- sources: bfloat16 [32768, 512], P(('cluster', 'row')), may hold values from -12 to 12
- targets: bfloat16 [32768, 512], P(('cluster', 'row')), may hold values from -12 to 12
- source_order: int32 [32768], P(('cluster', 'row')), may hold values from 0 to 255, as said below
- target_order: int32 [32768], P(('cluster', 'row')), may hold values from 0 to 255, as said below
Outputs:
- source_map: bfloat16 [32768, 512], P(('cluster', 'row'))
- target_map: bfloat16 [32768, 512], P(('cluster', 'row'))
Inputs may be any that keep to these rules, and one draw needn't show every extreme that they name: `source_order`: in each aligned block of 256 consecutive rows every value appears exactly once, so each block holds 32 source rows of every co-cluster. `target_order`: in each aligned block of 256 consecutive rows every value appears exactly once, so each block holds 32 target rows of every co-cluster.
All inputs are finite; a program needn't handle non-finite values.
Results may differ from a plain program's by a relative error of at most 0.01.
Values may be sent and summed in bfloat16 or wider, within the bound.
No kernel may reach another device: no remote copies, remote signals or barrier semaphores. Data moves between devices by JAX's collectives and lax.ppermute only.
A program may use at most 64 MiB of HBM per device.

v0:
```python
import math
import jax
import jax.numpy as jnp
from jax import lax
from jax.sharding import PartitionSpec as P

ITERS = 3
entropy_weight = 0.02


def square_sums(matrix):
    widened = matrix.astype(jnp.float32)
    return jnp.sum(widened * widened, axis=1)


def cost_panel(source_rows, source_norms, target_rows, target_norms):
    inner = jnp.einsum("id,jd->ij", source_rows, target_rows, preferred_element_type=jnp.float32)
    return (source_norms[:, None] + target_norms[None, :] - 2.0 * inner) / source_rows.shape[1]


def into_slots(ordering, matrix):
    positions = jnp.arange(matrix.shape[0], dtype=jnp.int32)
    selector = (positions[:, None] == ordering[None, :]).astype(jnp.bfloat16)
    return jnp.dot(selector, matrix, preferred_element_type=jnp.float32).astype(jnp.bfloat16)


def out_of_slots(ordering, matrix):
    positions = jnp.arange(matrix.shape[0], dtype=jnp.int32)
    selector = (ordering[:, None] == positions[None, :]).astype(jnp.bfloat16)
    return jnp.dot(selector, matrix, preferred_element_type=jnp.float32).astype(jnp.bfloat16)


def shards(sources, targets, source_order, target_order):
    rows_dev = sources.shape[0]
    width = sources.shape[1]
    sent_sources = into_slots(source_order, sources)
    sent_targets = into_slots(target_order, targets)
    local_sources, local_targets = (
        lax.all_to_all(sent_sources, "cluster", split_axis=0, concat_axis=0, tiled=True),
        lax.all_to_all(sent_targets, "cluster", split_axis=0, concat_axis=0, tiled=True),
    )
    cluster_targets = lax.all_gather(local_targets, "row", axis=0, tiled=True)
    columns = cluster_targets.shape[0]
    span = 512
    pieces = columns // span
    target_norms = square_sums(cluster_targets)
    target_blocks = cluster_targets.reshape(pieces, span, width)
    norm_blocks = target_norms.reshape(pieces, span)
    source_norms = square_sums(local_sources)
    log_mass = -math.log(columns)

    def row_lse(potential):

        def row_advance(carry, item):
            running, totals = carry
            block, block_norms, block_potential = item
            scores = (
                block_potential[None, :]
                - cost_panel(local_sources, source_norms, block, block_norms)
            ) / entropy_weight
            highest = jnp.maximum(running, jnp.max(scores, axis=1))
            totals = totals * jnp.exp(running - highest) + jnp.sum(
                jnp.exp(scores - highest[:, None]), axis=1
            )
            return ((highest, totals), None)

        start = (jnp.full((rows_dev,), -jnp.inf, jnp.float32), jnp.zeros((rows_dev,), jnp.float32))
        (running, totals), unused = lax.scan(
            row_advance, start, (target_blocks, norm_blocks, potential.reshape(pieces, span))
        )
        return running + jnp.log(totals)

    def column_lse(source_potential):

        def column_advance(carry, item):
            block, block_norms = item
            scores = (
                source_potential[:, None]
                - cost_panel(local_sources, source_norms, block, block_norms)
            ) / entropy_weight
            highest = jnp.max(scores, axis=0)
            return (carry, (highest, jnp.sum(jnp.exp(scores - highest[None, :]), axis=0)))

        unused, (peaks, totals) = lax.scan(column_advance, 0, (target_blocks, norm_blocks))
        peaks = peaks.reshape(-1)
        totals = totals.reshape(-1)
        highest = lax.pmax(peaks, "row")
        summed = lax.psum(totals * jnp.exp(peaks - highest), "row")
        return highest + jnp.log(summed)

    target_potential = jnp.zeros((columns,), jnp.float32)
    for repeat in range(ITERS):
        source_potential = entropy_weight * (log_mass - row_lse(target_potential))
        column_norm = column_lse(source_potential)
        target_potential = entropy_weight * (log_mass - column_norm)
    block = cluster_targets
    block_norms = target_norms
    scores = (
        source_potential[:, None] - cost_panel(local_sources, source_norms, block, block_norms)
    ) / entropy_weight
    weights = jnp.exp(scores - column_norm[None, :]).astype(jnp.bfloat16)
    target_map = lax.psum_scatter(
        jnp.einsum("ij,id->jd", weights, local_sources, preferred_element_type=jnp.float32).astype(
            jnp.bfloat16
        ),
        "row",
        scatter_dimension=0,
        tiled=True,
    )
    row_norm = row_lse(target_potential)

    def accumulate(carry, item):
        block, block_norms, block_potential = item
        scores = (
            block_potential[None, :] - cost_panel(local_sources, source_norms, block, block_norms)
        ) / entropy_weight
        weights = jnp.exp(scores - row_norm[:, None]).astype(jnp.bfloat16)
        return (carry + jnp.dot(weights, block, preferred_element_type=jnp.float32), None)

    source_sums, unused = lax.scan(
        accumulate,
        jnp.zeros((rows_dev, width), jnp.float32),
        (target_blocks, norm_blocks, target_potential.reshape(pieces, span)),
    )
    source_map = source_sums.astype(jnp.bfloat16)
    back_sources, back_targets = (
        lax.all_to_all(source_map, "cluster", split_axis=0, concat_axis=0, tiled=True),
        lax.all_to_all(target_map, "cluster", split_axis=0, concat_axis=0, tiled=True),
    )
    return (out_of_slots(source_order, back_sources), out_of_slots(target_order, back_targets))


def solution(mesh):
    return jax.shard_map(
        shards,
        mesh=mesh,
        in_specs=(
            P(("cluster", "row"), None),
            P(("cluster", "row"), None),
            P(("cluster", "row")),
            P(("cluster", "row")),
        ),
        out_specs=(P(("cluster", "row"), None), P(("cluster", "row"), None)),
        check_vma=False,
    )
```

profile of v0, /device:TPU:1, one launch (start us, length us, event | category | flops | bytes accessed | tf_op | source)
XLA Modules:
  0.0 678.2 jit_solution(1268138748987792291)
XLA Ops:
  9.0 12.2 %all_to_all.48 = bf16[8,32,512]{2,1,0:T(8,128)(2,1)} all-to-all(bf16[8,32,512]{2,1,0:T(8,128)(2,1)S(1)} %bitcast.260), channel_id=1, replica_groups=mesh['cluster'=8,'row'=16] {'cluster'}, dimensions={0} | all-to-all | bytes 524288 | tf_op jit(solution)/shard_map/all_to_all | solution.py:40
  21.2 1.9 convolution_convert_fusion.4
  23.1 4.4 all-to-all-start
  27.6 6.4 all-to-all-done
  34.2 39.4 %all-gather.2.cloned.1.call-done = bf16[4096,512]{1,0:T(8,128)(2,1)} async-done(((bf16[256,512]{1,0:T(8,128)(2,1)}), bf16[4096,512]{1,0:T(8,128)(2,1)}) %all-gather.2.cloned.1.call-update) | async-done | bytes 4194320 | tf_op jit(solution)/shard_map/all_gather | solution.py:42
  73.6 3.1 multiply_reduce_fusion
  76.7 12.7 %while.102 = (s32[]{:T(128)}, f32[256]{0:T(256)S(1)}, f32[256]{0:T(256)S(1)}, f32[256]{0:T(256)S(1)}, f32[8,512]{1,0:T(8,128)S(1)}, /*index=5*/bf16[8,512,512]{2...) while((s32[]{:T(128)}, f32[256]{0:T(256)S(1)}, f32[256]{0:T(256)S(1)}, ...), condition=%wide.region_5.6_spmd.clone, body=%wide.region_2.5_spmd.clone.sunk | while | flops 135398656 | bytes 1856108 | solution.py:68
  89.5 13.7 %while.99 = (s32[]{:T(128)}, f32[8,512]{1,0:T(8,128)S(1)}, f32[8,512]{1,0:T(8,128)S(1)}, f32[256]{0:T(256)S(1)}, f32[256]{0:T(256)S(1)}, /*index=5*/f32[8,512]{1...) while((s32[]{:T(128)}, f32[8,512]{1,0:T(8,128)S(1)}, ...), condition=%wide.region_9.10_spmd, body=%wide.region_6.9_spmd.sunk | while | flops 135396352 | bytes 1858161 | solution.py:84
  89.5 1.4 fusion.151
  91.2 1.4 fusion.151
  92.9 1.4 fusion.151
  94.6 1.4 fusion.151
  96.4 1.4 fusion.151
  98.1 1.4 fusion.151
  99.8 1.4 fusion.151
  101.5 1.4 fusion.151
  103.2 58.3 %pmax.21 = f32[4096]{0:T(1024)S(1)} all-reduce(f32[4096]{0:T(1024)S(1)} %bitcast.268), channel_id=1, replica_groups=mesh['cluster'=8,'row'=16] {'row'}, use_global_device_ids=true, to_apply=%region_10.11 | all-reduce | flops 4096 | bytes 32768 | tf_op jit(solution)/shard_map/pmax | solution.py:87
  161.5 55.6 %psum.21 = f32[4096]{0:T(1024)S(1)} all-reduce(f32[4096]{0:T(1024)S(1)} %exponential_multiply_fusion.2), channel_id=1, replica_groups=mesh['cluster'=8,'row'=16] {'row'}, use_global_device_ids=true, to_apply=%region_11.12 | all-reduce | flops 4096 | bytes 32768 | tf_op jit(solution)/shard_map/psum | solution.py:88
  217.1 12.8 %while.103 = (s32[]{:T(128)}, f32[256]{0:T(256)S(1)}, f32[256]{0:T(256)S(1)}, f32[8,512]{1,0:T(8,128)S(1)}, f32[256]{0:T(256)S(1)}, /*index=5*/f32[8,512]{1,0:T(...) while((s32[]{:T(128)}, f32[256]{0:T(256)S(1)}, ...), condition=%wide.region_15.16_spmd.clone, body=%wide.region_12.15_spmd.clone.sunk | while | flops 135398656 | bytes 1862260 | solution.py:68
  217.2 1.4 fusion.161
  218.8 1.4 fusion.161
  223.6 1.4 fusion.161
  228.4 1.4 fusion.161
  230.0 13.7 %while.100 = (s32[]{:T(128)}, f32[8,512]{1,0:T(8,128)S(1)}, f32[8,512]{1,0:T(8,128)S(1)}, f32[256]{0:T(256)S(1)}, f32[256]{0:T(256)S(1)}, /*index=5*/f32[8,512]{...) while((s32[]{:T(128)}, f32[8,512]{1,0:T(8,128)S(1)}, ...), condition=%wide.region_19.20_spmd, body=%wide.region_16.19_spmd.sunk | while | flops 135396352 | bytes 1858161 | solution.py:84
  230.0 1.4 fusion.153
  231.7 1.4 fusion.153
  233.5 1.4 fusion.153
  235.2 1.4 fusion.153
  236.9 1.4 fusion.153
  238.6 1.4 fusion.153
  240.3 1.4 fusion.153
  242.0 1.4 fusion.153
  243.7 55.6 %pmax.22 = f32[4096]{0:T(1024)S(1)} all-reduce(f32[4096]{0:T(1024)S(1)} %bitcast.270), channel_id=1, replica_groups=mesh['cluster'=8,'row'=16] {'row'}, use_global_device_ids=true, to_apply=%region_20.21 | all-reduce | flops 4096 | bytes 32768 | tf_op jit(solution)/shard_map/pmax | solution.py:87
  299.4 56.0 %psum.22 = f32[4096]{0:T(1024)S(1)} all-reduce(f32[4096]{0:T(1024)S(1)} %exponential_multiply_fusion.1), channel_id=1, replica_groups=mesh['cluster'=8,'row'=16] {'row'}, use_global_device_ids=true, to_apply=%region_21.22 | all-reduce | flops 4096 | bytes 32768 | tf_op jit(solution)/shard_map/psum | solution.py:88
  355.3 12.8 %while.104 = (s32[]{:T(128)}, f32[256]{0:T(256)S(1)}, f32[256]{0:T(256)S(1)}, f32[8,512]{1,0:T(8,128)S(1)}, f32[256]{0:T(256)S(1)}, /*index=5*/f32[8,512]{1,0:T(...) while((s32[]{:T(128)}, f32[256]{0:T(256)S(1)}, ...), condition=%wide.region_25.26_spmd.clone, body=%wide.region_22.25_spmd.clone.sunk | while | flops 135398656 | bytes 1862260 | solution.py:68
  361.8 1.4 fusion.165
  368.2 13.7 %while.101 = (s32[]{:T(128)}, f32[8,512]{1,0:T(8,128)S(1)}, f32[8,512]{1,0:T(8,128)S(1)}, f32[256]{0:T(256)S(1)}, f32[256]{0:T(256)S(1)}, /*index=5*/f32[8,512]{...) while((s32[]{:T(128)}, f32[8,512]{1,0:T(8,128)S(1)}, ...), condition=%wide.region_29.30_spmd, body=%wide.region_26.29_spmd.sunk | while | flops 135396352 | bytes 1858161 | solution.py:84
  368.2 1.4 fusion.155
  369.9 1.4 fusion.155
  371.7 1.4 fusion.155
  373.4 1.4 fusion.155
  375.1 1.4 fusion.155
  376.8 1.4 fusion.155
  378.5 1.4 fusion.155
  380.3 1.4 fusion.155
  382.0 55.6 %pmax.23 = f32[4096]{0:T(1024)S(1)} all-reduce(f32[4096]{0:T(1024)S(1)} %bitcast.272), channel_id=1, replica_groups=mesh['cluster'=8,'row'=16] {'row'}, use_global_device_ids=true, to_apply=%region_30.31 | all-reduce | flops 4096 | bytes 32768 | tf_op jit(solution)/shard_map/pmax | solution.py:87
  437.6 55.6 %psum.23 = f32[4096]{0:T(1024)S(1)} all-reduce(f32[4096]{0:T(1024)S(1)} %exponential_multiply_fusion), channel_id=1, replica_groups=mesh['cluster'=8,'row'=16] {'row'}, use_global_device_ids=true, to_apply=%region_31.32 | all-reduce | flops 4096 | bytes 32768 | tf_op jit(solution)/shard_map/psum | solution.py:88
  493.2 7.0 %convolution_convert_fusion = bf16[4096,512]{1,0:T(8,128)(2,1)} fusion(bf16[256,512]{1,0:T(8,128)(2,1)S(1)} %get-tuple-element.1322, bf16[4096,512]{1,0:T(8,128)(2,1)} %bitcast.254, f32[4096]{0:T(1024)S(1)} %get-tuple-element.614, f32[4096]{0:T(1024)S(1)} %multiply_reduce_fusion, f32[256]{0:T(256)S(1)} %get-tuple-element.1343, f32[256]{0:T(256)S(1)} %get-tuple-element.1345), kind=kOutput, calls=%fused_computation.123 | convolution fusion | flops 2157969408 | bytes 8685568 | tf_op jit(solution)/shard_map/ij,id->jd/dot_general | solution.py:103
  500.2 12.8 %while.105 = (s32[]{:T(128)}, f32[256]{0:T(256)S(1)}, f32[256]{0:T(256)S(1)}, f32[8,512]{1,0:T(8,128)S(1)}, f32[256]{0:T(256)S(1)}, /*index=5*/f32[8,512]{1,0:T(...) while((s32[]{:T(128)}, f32[256]{0:T(256)S(1)}, ...), condition=%wide.region_35.36_spmd.clone, body=%wide.region_32.35_spmd.clone.sunk | while | flops 135398656 | bytes 1862260 | solution.py:68
  503.5 1.4 fusion.169
  508.3 1.4 fusion.169
  513.1 15.4 %while.106 = (s32[]{:T(128)}, f32[256,512]{1,0:T(8,128)S(1)}, f32[8,512]{1,0:T(8,128)S(1)}, f32[256]{0:T(256)S(1)}, f32[8,512]{1,0:T(8,128)S(1)}, /*index=5*/bf1...) while((s32[]{:T(128)}, f32[256,512]{1,0:T(8,128)S(1)}, ...), condition=%wide.region_37.38_spmd.clone, body=%wide.region_36.37_spmd.clone.sunk | while | flops 269746176 | bytes 2374771 | solution.py:120
  513.1 1.9 convolution_add_fusion.2
  515.1 1.9 convolution_add_fusion.2
  517.0 1.9 convolution_add_fusion.2
  518.9 1.9 convolution_add_fusion.2
  520.8 1.9 convolution_add_fusion.2
  522.7 1.9 convolution_add_fusion.2
  524.7 1.9 convolution_add_fusion.2
  526.6 1.9 convolution_add_fusion.2
  528.5 94.9 %all_to_all.49 = bf16[8,32,512]{2,1,0:T(8,128)(2,1)S(1)} all-to-all(bf16[8,32,512]{2,1,0:T(8,128)(2,1)S(1)} %bitcast.255), channel_id=1, replica_groups=mesh['cluster'=8,'row'=16] {'cluster'}, dimensions={0} | all-to-all | bytes 524288 | tf_op jit(solution)/shard_map/all_to_all | solution.py:127
  623.4 33.8 %reduce-scatter.2.cloned.1.call-done = bf16[256,512]{1,0:T(8,128)(2,1)} async-done(((bf16[4096,512]{1,0:T(8,128)(2,1)}), bf16[256,512]{1,0:T(8,128)(2,1)}) %reduce-scatter.2.cloned.1.call-update) | async-done | bytes 262160 | tf_op jit(solution)/shard_map/reduce_scatter | solution.py:102
  657.2 6.7 all-to-all-start.3
  664.9 5.5 all-to-all-done.3
  (340 shorter events, 50.0 us)
Async XLA Ops:
  7.2 1.0 copy-start
  7.2 66.4 %all-gather.2.cloned.1.call-start = ((), (), s32[]{:S(2)}) async-start(), calls=%async_computation.5 | async-start | bytes 4456448 | tf_op jit(solution)/shard_map/all_gather | solution.py:42
  23.1 10.8 %all-to-all-start = ((bf16[8,32,512]{2,1,0:T(8,128)(2,1)}), bf16[8,32,512]{2,1,0:T(8,128)(2,1)S(1)}, u32[]{:S(2)}, u32[]{:S(2)}) async-start(bf16[8,32,512]{2,1,0:T(8,128)(2,1)} %bitcast.15), calls=%async_computation | async-start | bytes 524288 | tf_op jit(solution)/shard_map/all_to_all | solution.py:39
  27.5 629.7 %reduce-scatter.2.cloned.1.call-start = ((), (), s32[]{:S(2)}) async-start(), calls=%async_computation.6 | async-start | bytes 4456448 | tf_op jit(solution)/shard_map/reduce_scatter | solution.py:102
  513.1 150.8 %copy-start.1 = (s32[256]{0:T(256)S(1)}, s32[256]{0:T(256)}, u32[]{:S(2)}) copy-start(s32[256]{0:T(256)} %param.22) | copy-start | bytes 3076
  513.1 157.3 %copy-start.2 = (s32[256]{0:T(256)S(1)}, s32[256]{0:T(256)}, u32[]{:S(2)}) copy-start(s32[256]{0:T(256)} %param.23) | copy-start | bytes 3076
  657.2 13.2 %all-to-all-start.3 = ((bf16[8,32,512]{2,1,0:T(8,128)(2,1)}), bf16[8,32,512]{2,1,0:T(8,128)(2,1)S(1)}, u32[]{:S(2)}, u32[]{:S(2)}) async-start(bf16[8,32,512]{2,1,0:T(8,128)(2,1)} %bitcast.261), calls=%async_computation.4 | async-start | bytes 524288 | tf_op jit(solution)/shard_map/all_to_all | solution.py:128
Sparse Core Ops, SparseCore 0:
  21.3 52.2 all-gather.1
  500.3 156.7 reduce-scatter.1
where the time goes:
time: 682 us; the launch traced here: 678 us
  blocking collectives  444 us (65%)
  matrix products  106 us (16%)
  waiting for transfers between devices  85.2 us (12%)
  between operations  14.3 us (2%)
  starting transfers between devices  11.1 us (2%)
  other arithmetic  10.7 us (2%)
    pmax x3, blocking collectives, column_lse(): highest = lax.pmax(peaks, 'row')  170 us
    psum x3, blocking collectives, column_lse(): summed = lax.psum(totals * jnp.exp(peaks - highest), 'row')  167 us
    all_to_all x1, blocking collectives, shards(): lax.all_to_all(source_map, 'cluster', split_axis=0, concat_axis=0, tiled=...  94.9 us
    dot_general x56, matrix products, cost_panel(): jnp.einsum('id,jd->ij', source_rows, target_rows, preferred_element_type=...  79.3 us
    all_gather x1, waiting for transfers between devices, shards(): cluster_targets = lax.all_gather(local_targets, 'row', axis=0, tiled=True)  39.4 us
    reduce_scatter x1, waiting for transfers between devices, shards(): lax.psum_scatter(jnp.einsum('ij,id->jd', weights, local_sources, preferre...  33.8 us
    dot_general x8, matrix products, accumulate(): jnp.dot(weights, block, preferred_element_type=jnp.float32)  15 us
  transfers between devices with their start and end apart: 4, of which 4 were waited for; matrix products, arithmetic and copies ran while one was open for 5% of the time, Pallas kernels for 0%

commit v1 on v0

--- a/solution.py
+++ b/solution.py
@@ -39,7 +39,9 @@
         lax.all_to_all(sent_sources, "cluster", split_axis=0, concat_axis=0, tiled=True),
         lax.all_to_all(sent_targets, "cluster", split_axis=0, concat_axis=0, tiled=True),
     )
-    cluster_targets = lax.all_gather(local_targets, "row", axis=0, tiled=True)
+    cluster_targets = jnp.concatenate(
+        lax.all_to_all(jnp.stack([local_targets] * lax.axis_size("row")), "row", 0, 0), axis=0
+    )
     columns = cluster_targets.shape[0]
     span = 512
     pieces = columns // span

time: 682 us -> 711 us (1.043)
  waiting for transfers between devices: 85.2 us -> 106 us
  starting transfers between devices: 11.1 us -> 20.4 us
    all_to_all x1 -> x2, waiting for transfers between devices: 6.43 us -> 66.5 us  [the longest x1 61.2 us: shards(): lax.all_to_all(jnp.stack([local_targets] * lax.axis_size('row')), 'row',...]
    all_gather x1 -> x0, waiting for transfers between devices: 39.4 us -> none  [shards(): cluster_targets = lax.all_gather(local_targets, 'row', axis=0, tiled=True)]
    all_to_all x1 -> x2, starting transfers between devices: 4.35 us -> 13.6 us  [the longest x1 7.82 us: shards(): lax.all_to_all(jnp.stack([local_targets] * lax.axis_size('row')), 'row',...]
  transfers between devices with their start and end apart: 4 -> 4, of which waited for: 4 -> 4; matrix products, arithmetic and copies ran while one was open for 5% -> 4% of each run, Pallas kernels for 0% -> 0%
where the time goes in v1:
time: 711 us; the launch traced here: 707 us
  blocking collectives  440 us (62%)
  matrix products  106 us (15%)
  waiting for transfers between devices  106 us (15%)
  starting transfers between devices  20.4 us (3%)
  between operations  14.4 us (2%)
  other arithmetic  10.7 us (2%)
    pmax x3, blocking collectives, column_lse(): highest = lax.pmax(peaks, 'row')  169 us
    psum x3, blocking collectives, column_lse(): summed = lax.psum(totals * jnp.exp(peaks - highest), 'row')  168 us
    all_to_all x1, blocking collectives, shards(): lax.all_to_all(source_map, 'cluster', split_axis=0, concat_axis=0, tiled=...  93.7 us
    dot_general x56, matrix products, cost_panel(): jnp.einsum('id,jd->ij', source_rows, target_rows, preferred_element_type=...  79.4 us
    all_to_all x1, waiting for transfers between devices, shards(): lax.all_to_all(jnp.stack([local_targets] * lax.axis_size('row')), 'row',...  61.2 us
    reduce_scatter x1, waiting for transfers between devices, shards(): lax.psum_scatter(jnp.einsum('ij,id->jd', weights, local_sources, preferre...  33.7 us
    dot_general x8, matrix products, accumulate(): jnp.dot(weights, block, preferred_element_type=jnp.float32)  15 us
  transfers between devices with their start and end apart: 4, of which 4 were waited for; matrix products, arithmetic and copies ran while one was open for 4% of the time, Pallas kernels for 0%

profile of v1, /device:TPU:1, one launch (start us, length us, event | category | flops | bytes accessed | tf_op | source)
XLA Modules:
  0.0 707.3 jit_solution(3248353970272856492)
XLA Ops:
  8.1 1.6 convolution_convert_fusion.3
  9.7 5.8 all-to-all-start.1
  16.7 5.3 all-to-all-done.1
  22.0 9.9 %all_to_all.50 = bf16[8,32,512]{2,1,0:T(8,128)(2,1)S(1)} all-to-all(bf16[8,32,512]{2,1,0:T(8,128)(2,1)S(1)} %bitcast.261), channel_id=1, replica_groups=mesh['cluster'=8,'row'=16] {'cluster'}, dimensions={0} | all-to-all | bytes 524288 | tf_op jit(solution)/shard_map/all_to_all | solution.py:39
  31.9 2.4 stack.5
  34.3 7.8 %all-to-all-start.2 = ((bf16[16,256,512]{2,1,0:T(8,128)(2,1)}), bf16[16,256,512]{2,1,0:T(8,128)(2,1)}, u32[]{:S(2)}, u32[]{:S(2)}) async-start(bf16[16,256,512]{2,1,0:T(8,128)(2,1)} %stack.5), calls=%async_computation.2 | async-start | bytes 8388608 | tf_op jit(solution)/shard_map/all_to_all | solution.py:43
  42.4 61.2 %all-to-all-done.2 = bf16[16,256,512]{2,1,0:T(8,128)(2,1)} async-done(((bf16[16,256,512]{2,1,0:T(8,128)(2,1)}), bf16[16,256,512]{2,1,0:T(8,128)(2,1)}, u32[]{:S(2)}, u32[]{:S(2)}) %all-to-all-start.2) | async-done | bytes 4194336 | tf_op jit(solution)/shard_map/all_to_all | solution.py:43
  103.7 3.1 multiply_reduce_fusion
  106.8 12.7 %while.102 = (s32[]{:T(128)}, f32[256]{0:T(256)S(1)}, f32[256]{0:T(256)S(1)}, f32[256]{0:T(256)S(1)}, f32[8,512]{1,0:T(8,128)S(1)}, /*index=5*/bf16[8,512,512]{2...) while((s32[]{:T(128)}, f32[256]{0:T(256)S(1)}, f32[256]{0:T(256)S(1)}, ...), condition=%wide.region_5.6_spmd.clone, body=%wide.region_2.5_spmd.clone.sunk | while | flops 135398656 | bytes 1856108 | solution.py:70
  119.5 13.7 %while.99 = (s32[]{:T(128)}, f32[8,512]{1,0:T(8,128)S(1)}, f32[8,512]{1,0:T(8,128)S(1)}, f32[256]{0:T(256)S(1)}, f32[256]{0:T(256)S(1)}, /*index=5*/f32[8,512]{1...) while((s32[]{:T(128)}, f32[8,512]{1,0:T(8,128)S(1)}, ...), condition=%wide.region_9.10_spmd, body=%wide.region_6.9_spmd.sunk | while | flops 135396352 | bytes 1858161 | solution.py:86
  119.5 1.4 fusion.151
  121.3 1.4 fusion.151
  123.0 1.4 fusion.151
  124.7 1.4 fusion.151
  126.4 1.4 fusion.151
  128.1 1.4 fusion.151
  129.9 1.4 fusion.151
  131.6 1.4 fusion.151
  133.3 57.7 %pmax.21 = f32[4096]{0:T(1024)S(1)} all-reduce(f32[4096]{0:T(1024)S(1)} %bitcast.270), channel_id=1, replica_groups=mesh['cluster'=8,'row'=16] {'row'}, use_global_device_ids=true, to_apply=%region_10.11 | all-reduce | flops 4096 | bytes 32768 | tf_op jit(solution)/shard_map/pmax | solution.py:89
  191.0 55.9 %psum.21 = f32[4096]{0:T(1024)S(1)} all-reduce(f32[4096]{0:T(1024)S(1)} %exponential_multiply_fusion.2), channel_id=1, replica_groups=mesh['cluster'=8,'row'=16] {'row'}, use_global_device_ids=true, to_apply=%region_11.12 | all-reduce | flops 4096 | bytes 32768 | tf_op jit(solution)/shard_map/psum | solution.py:90
  247.0 12.8 %while.103 = (s32[]{:T(128)}, f32[256]{0:T(256)S(1)}, f32[256]{0:T(256)S(1)}, f32[8,512]{1,0:T(8,128)S(1)}, f32[256]{0:T(256)S(1)}, /*index=5*/f32[8,512]{1,0:T(...) while((s32[]{:T(128)}, f32[256]{0:T(256)S(1)}, ...), condition=%wide.region_15.16_spmd.clone, body=%wide.region_12.15_spmd.clone.sunk | while | flops 135398656 | bytes 1862260 | solution.py:70
  247.0 1.4 fusion.161
  251.8 1.4 fusion.161
  256.6 1.4 fusion.161
  259.9 13.7 %while.100 = (s32[]{:T(128)}, f32[8,512]{1,0:T(8,128)S(1)}, f32[8,512]{1,0:T(8,128)S(1)}, f32[256]{0:T(256)S(1)}, f32[256]{0:T(256)S(1)}, /*index=5*/f32[8,512]{...) while((s32[]{:T(128)}, f32[8,512]{1,0:T(8,128)S(1)}, ...), condition=%wide.region_19.20_spmd, body=%wide.region_16.19_spmd.sunk | while | flops 135396352 | bytes 1858161 | solution.py:86
  259.9 1.4 fusion.153
  261.6 1.4 fusion.153
  263.3 1.4 fusion.153
  265.0 1.4 fusion.153
  266.7 1.4 fusion.153
  268.5 1.4 fusion.153
  270.2 1.4 fusion.153
  271.9 1.4 fusion.153
  273.6 55.8 %pmax.22 = f32[4096]{0:T(1024)S(1)} all-reduce(f32[4096]{0:T(1024)S(1)} %bitcast.272), channel_id=1, replica_groups=mesh['cluster'=8,'row'=16] {'row'}, use_global_device_ids=true, to_apply=%region_20.21 | all-reduce | flops 4096 | bytes 32768 | tf_op jit(solution)/shard_map/pmax | solution.py:89
  329.4 56.1 %psum.22 = f32[4096]{0:T(1024)S(1)} all-reduce(f32[4096]{0:T(1024)S(1)} %exponential_multiply_fusion.1), channel_id=1, replica_groups=mesh['cluster'=8,'row'=16] {'row'}, use_global_device_ids=true, to_apply=%region_21.22 | all-reduce | flops 4096 | bytes 32768 | tf_op jit(solution)/shard_map/psum | solution.py:90
  385.6 12.8 %while.104 = (s32[]{:T(128)}, f32[256]{0:T(256)S(1)}, f32[256]{0:T(256)S(1)}, f32[8,512]{1,0:T(8,128)S(1)}, f32[256]{0:T(256)S(1)}, /*index=5*/f32[8,512]{1,0:T(...) while((s32[]{:T(128)}, f32[256]{0:T(256)S(1)}, ...), condition=%wide.region_25.26_spmd.clone, body=%wide.region_22.25_spmd.clone.sunk | while | flops 135398656 | bytes 1862260 | solution.py:70
  388.8 1.4 fusion.165
  398.4 13.7 %while.101 = (s32[]{:T(128)}, f32[8,512]{1,0:T(8,128)S(1)}, f32[8,512]{1,0:T(8,128)S(1)}, f32[256]{0:T(256)S(1)}, f32[256]{0:T(256)S(1)}, /*index=5*/f32[8,512]{...) while((s32[]{:T(128)}, f32[8,512]{1,0:T(8,128)S(1)}, ...), condition=%wide.region_29.30_spmd, body=%wide.region_26.29_spmd.sunk | while | flops 135396352 | bytes 1858161 | solution.py:86
  398.5 1.4 fusion.155
  400.2 1.4 fusion.155
  401.9 1.4 fusion.155
  403.6 1.4 fusion.155
  405.3 1.4 fusion.155
  407.1 1.4 fusion.155
  408.8 1.4 fusion.155
  410.5 1.4 fusion.155
  412.2 55.6 %pmax.23 = f32[4096]{0:T(1024)S(1)} all-reduce(f32[4096]{0:T(1024)S(1)} %bitcast.274), channel_id=1, replica_groups=mesh['cluster'=8,'row'=16] {'row'}, use_global_device_ids=true, to_apply=%region_30.31 | all-reduce | flops 4096 | bytes 32768 | tf_op jit(solution)/shard_map/pmax | solution.py:89
  467.9 55.6 %psum.23 = f32[4096]{0:T(1024)S(1)} all-reduce(f32[4096]{0:T(1024)S(1)} %exponential_multiply_fusion), channel_id=1, replica_groups=mesh['cluster'=8,'row'=16] {'row'}, use_global_device_ids=true, to_apply=%region_31.32 | all-reduce | flops 4096 | bytes 32768 | tf_op jit(solution)/shard_map/psum | solution.py:90
  523.5 7.0 convolution_convert_fusion
  530.5 12.8 %while.105 = (s32[]{:T(128)}, f32[256]{0:T(256)S(1)}, f32[256]{0:T(256)S(1)}, f32[8,512]{1,0:T(8,128)S(1)}, f32[256]{0:T(256)S(1)}, /*index=5*/f32[8,512]{1,0:T(...) while((s32[]{:T(128)}, f32[256]{0:T(256)S(1)}, ...), condition=%wide.region_35.36_spmd.clone, body=%wide.region_32.35_spmd.clone.sunk | while | flops 135398656 | bytes 1862260 | solution.py:70
  537.0 1.4 fusion.169
  543.4 15.4 %while.106 = (s32[]{:T(128)}, f32[256,512]{1,0:T(8,128)S(1)}, f32[8,512]{1,0:T(8,128)S(1)}, f32[256]{0:T(256)S(1)}, f32[8,512]{1,0:T(8,128)S(1)}, /*index=5*/bf1...) while((s32[]{:T(128)}, f32[256,512]{1,0:T(8,128)S(1)}, ...), condition=%wide.region_37.38_spmd.clone, body=%wide.region_36.37_spmd.clone.sunk | while | flops 269746176 | bytes 2374771 | solution.py:122
  543.4 1.9 convolution_add_fusion.2
  545.3 1.9 convolution_add_fusion.2
  547.2 1.9 convolution_add_fusion.2
  549.2 1.9 convolution_add_fusion.2
  551.1 1.9 convolution_add_fusion.2
  553.0 1.9 convolution_add_fusion.2
  555.0 1.9 convolution_add_fusion.2
  556.9 1.9 convolution_add_fusion.2
  558.8 93.7 %all_to_all.51 = bf16[8,32,512]{2,1,0:T(8,128)(2,1)S(1)} all-to-all(bf16[8,32,512]{2,1,0:T(8,128)(2,1)S(1)} %bitcast.257), channel_id=1, replica_groups=mesh['cluster'=8,'row'=16] {'cluster'}, dimensions={0} | all-to-all | bytes 524288 | tf_op jit(solution)/shard_map/all_to_all | solution.py:129
  652.5 33.7 %reduce-scatter.2.cloned.1.call-done = bf16[256,512]{1,0:T(8,128)(2,1)} async-done(((bf16[4096,512]{1,0:T(8,128)(2,1)}), bf16[256,512]{1,0:T(8,128)(2,1)}) %reduce-scatter.2.cloned.1.call-update) | async-done | bytes 262160 | tf_op jit(solution)/shard_map/reduce_scatter | solution.py:104
  686.3 6.7 all-to-all-start.4
  693.9 5.5 all-to-all-done.4
  (341 shorter events, 53.2 us)
Async XLA Ops:
  7.2 1.0 copy-start
  9.7 12.3 %all-to-all-start.1 = ((bf16[8,32,512]{2,1,0:T(8,128)(2,1)}), bf16[8,32,512]{2,1,0:T(8,128)(2,1)S(1)}, u32[]{:S(2)}, u32[]{:S(2)}) async-start(bf16[8,32,512]{2,1,0:T(8,128)(2,1)} %bitcast.16), calls=%async_computation.1 | async-start | bytes 524288 | tf_op jit(solution)/shard_map/all_to_all | solution.py:40
  34.3 69.4 %all-to-all-start.2 = ((bf16[16,256,512]{2,1,0:T(8,128)(2,1)}), bf16[16,256,512]{2,1,0:T(8,128)(2,1)}, u32[]{:S(2)}, u32[]{:S(2)}) async-start(bf16[16,256,512]{2,1,0:T(8,128)(2,1)} %stack.5), calls=%async_computation.2 | async-start | bytes 8388608 | tf_op jit(solution)/shard_map/all_to_all | solution.py:43
  42.1 644.1 %reduce-scatter.2.cloned.1.call-start = ((), (), s32[]{:S(2)}) async-start(), calls=%async_computation.6 | async-start | bytes 4456448 | tf_op jit(solution)/shard_map/reduce_scatter | solution.py:104
  543.4 149.6 %copy-start.1 = (s32[256]{0:T(256)S(1)}, s32[256]{0:T(256)}, u32[]{:S(2)}) copy-start(s32[256]{0:T(256)} %param.22) | copy-start | bytes 3076
  543.4 156.1 %copy-start.2 = (s32[256]{0:T(256)S(1)}, s32[256]{0:T(256)}, u32[]{:S(2)}) copy-start(s32[256]{0:T(256)} %param.23) | copy-start | bytes 3076
  686.3 13.2 %all-to-all-start.4 = ((bf16[8,32,512]{2,1,0:T(8,128)(2,1)}), bf16[8,32,512]{2,1,0:T(8,128)(2,1)S(1)}, u32[]{:S(2)}, u32[]{:S(2)}) async-start(bf16[8,32,512]{2,1,0:T(8,128)(2,1)} %bitcast.262), calls=%async_computation.5 | async-start | bytes 524288 | tf_op jit(solution)/shard_map/all_to_all | solution.py:130
Sparse Core Ops, SparseCore 0:
  530.6 155.5 reduce-scatter.1
